TPU v7x, 128 devices: a whole 4x4x4 slice. The times are simulated.
128 devices in a mesh: prow: 8 (over y, core), pcol: 16 (over x, z).
Axes of the slice: x: 4, y: 4, z: 4, core: 2. Of those that a mesh axis runs over, the one named last changes fastest.
Arguments:
- right_sides: bfloat16 [32768, 128], P(('prow', 'pcol')), may hold values from -6 to 6
- factor: bfloat16 [16, 16, 32, 8, 128, 128], P(None, 'pcol', None, 'prow'), may hold values from -0.046875 to 0.046875
- pattern: int32 [16, 16, 32, 8], P(None, 'pcol', None, 'prow'), may hold values 0 or 1
- lower_inverse: bfloat16 [16, 16, 128, 128], P(None, 'pcol'), may hold values from -0.5 to 0.5
- upper_inverse: bfloat16 [16, 16, 128, 128], P(None, 'pcol'), may hold values from -0.5 to 0.5
Outputs:
- solution: bfloat16 [32768, 128], P(('prow', 'pcol'))
All inputs are finite; a program needn't handle non-finite values. No bound on the sum of `pattern` on one device may be relied on, other than what follows from the above.
Results may differ from a plain program's by a relative error of at most 0.02.
Values may be sent and summed in bfloat16 or wider, within the bound.
A program may use at most 128 MiB of HBM per device.

v0:
```python
import jax
import jax.numpy as jnp
from jax import lax
from jax.sharding import PartitionSpec as P


def level_index(index_vals, node_count):
    bounds = (node_count // 2, 3 * node_count // 4, 7 * node_count // 8)
    result = jnp.zeros(index_vals.shape, jnp.int32)
    for edge_val in bounds:
        result = result + (index_vals >= edge_val).astype(jnp.int32)
    return result


def level_sums(
    blocks,
    pattern_loc,
    col_levels,
    solved_all,
    row_id,
    prow_n,
    row_start,
    row_end,
    col_start,
    col_end,
    level_id,
    upward,
):
    if col_end <= col_start:
        return None
    block_size = blocks.shape[2]
    rhs_count = solved_all.shape[2]
    grouped = solved_all.reshape(-1, prow_n, block_size, rhs_count)
    column_vals = lax.dynamic_index_in_dim(grouped, row_id, 1, keepdims=False)[col_start:col_end]
    levels_here = col_levels[col_start:col_end]
    if upward:
        order_mask = levels_here > level_id
    else:
        order_mask = levels_here < level_id
    keep_mask = (pattern_loc[row_start:row_end, col_start:col_end] > 0) & order_mask[None, :]
    masked = jnp.where(
        keep_mask[:, :, None, None],
        blocks[row_start:row_end, col_start:col_end],
        jnp.zeros((), jnp.bfloat16),
    )
    return jnp.einsum("ijab,jbn->ian", masked, column_vals, preferred_element_type=jnp.float32)


def finish_level(partial_value, base_rows, inverse_rows, pcol_n):
    row_count = base_rows.shape[0]
    block_size = base_rows.shape[1]
    rhs_count = base_rows.shape[2]
    if partial_value is None:
        remainder = base_rows
    else:
        summed = lax.psum(partial_value.astype(jnp.bfloat16), "prow").astype(jnp.float32)
        remainder = (base_rows.astype(jnp.float32) - summed).astype(jnp.bfloat16)
    solved = jnp.einsum(
        "iab,ibn->ian", inverse_rows, remainder, preferred_element_type=jnp.float32
    ).astype(jnp.bfloat16)
    gathered = lax.all_gather(solved[:, None], "pcol", axis=1, tiled=True)
    return gathered.reshape(row_count * pcol_n, block_size, rhs_count)


def on_device(right_sides, factor, pattern, lower_inverse, upper_inverse):
    prow_n = lax.axis_size("prow")
    pcol_n = lax.axis_size("pcol")
    row_id = lax.axis_index("prow")
    col_id = lax.axis_index("pcol")
    blocks = factor[:, 0, :, 0]
    pattern_loc = pattern[:, 0, :, 0]
    lower_rows = lower_inverse[:, 0]
    upper_rows = upper_inverse[:, 0]
    row_blocks = blocks.shape[0]
    col_blocks = blocks.shape[1]
    block_size = blocks.shape[2]
    rhs_count = right_sides.shape[1]
    node_count = row_blocks * pcol_n
    everything = lax.all_gather(right_sides, ("prow", "pcol"), axis=0, tiled=True)
    everything = everything.reshape(row_blocks, pcol_n, block_size, rhs_count)
    mine_right = lax.dynamic_index_in_dim(everything, col_id, 1, keepdims=False)
    col_levels = level_index(jnp.arange(col_blocks, dtype=jnp.int32) * prow_n + row_id, node_count)
    bounds = (0, row_blocks // 2, 3 * row_blocks // 4, 7 * row_blocks // 8, row_blocks)
    forward_vals = jnp.zeros((node_count, block_size, rhs_count), jnp.bfloat16)
    for level_id in range(4):
        row_start, row_end = (bounds[level_id], bounds[level_id + 1])
        col_end = min(col_blocks, -(-(row_start * pcol_n) // prow_n))
        partial_value = level_sums(
            blocks,
            pattern_loc,
            col_levels,
            forward_vals,
            row_id,
            prow_n,
            row_start,
            row_end,
            0,
            col_end,
            level_id,
            False,
        )
        solved = finish_level(
            partial_value, mine_right[row_start:row_end], lower_rows[row_start:row_end], pcol_n
        )
        forward_vals = lax.dynamic_update_slice_in_dim(forward_vals, solved, row_start * pcol_n, 0)
    forward_mine = lax.dynamic_index_in_dim(
        forward_vals.reshape(row_blocks, pcol_n, block_size, rhs_count), col_id, 1, keepdims=False
    )
    backward_vals = jnp.zeros((node_count, block_size, rhs_count), jnp.bfloat16)
    for level_id in (3, 2, 1, 0):
        row_start, row_end = (bounds[level_id], bounds[level_id + 1])
        col_start = row_end * pcol_n // prow_n
        partial_value = level_sums(
            blocks,
            pattern_loc,
            col_levels,
            backward_vals,
            row_id,
            prow_n,
            row_start,
            row_end,
            col_start,
            col_blocks,
            level_id,
            True,
        )
        solved = finish_level(
            partial_value, forward_mine[row_start:row_end], upper_rows[row_start:row_end], pcol_n
        )
        backward_vals = lax.dynamic_update_slice_in_dim(
            backward_vals, solved, row_start * pcol_n, 0
        )
    out_rows = right_sides.shape[0]
    device_id = row_id * pcol_n + col_id
    flat = backward_vals.reshape(node_count * block_size, rhs_count)
    return lax.dynamic_slice_in_dim(flat, device_id * out_rows, out_rows, 0)


def solution(mesh):
    placed = (
        P(("prow", "pcol"), None),
        P(None, "pcol", None, "prow", None, None),
        P(None, "pcol", None, "prow"),
        P(None, "pcol", None, None),
        P(None, "pcol", None, None),
    )
    return jax.shard_map(
        on_device, mesh=mesh, in_specs=placed, out_specs=P(("prow", "pcol"), None), check_vma=False
    )
```

profile of v0, /device:TPU:1, one launch (start us, length us, event | category | flops | bytes accessed | tf_op | source)
XLA Modules:
  0.0 902.1 jit_solution(18157509265006647587)
XLA Ops:
  7.3 76.5 %all-gather.18.cloned.1.call-done = bf16[32768,128]{1,0:T(8,128)(2,1)} async-done(((bf16[256,128]{1,0:T(8,128)(2,1)}), bf16[32768,128]{1,0:T(8,128)(2,1)}) %all-gather.18.cloned.1.call-update) | async-done | bytes 8388624 | tf_op jit(solution)/shard_map/all_gather | solution.py:79
  83.8 2.1 fusion.11
  86.8 52.0 %all-gather.20.cloned.1.call-done = bf16[8,2048,128]{1,2,0:T(8,128)(2,1)} async-done(((bf16[8,128,128]{1,2,0:T(8,128)(2,1)}), bf16[8,2048,128]{1,2,0:T(8,128)(2,1)}) %all-gather.20.cloned.1.call-update) | async-done | bytes 4194320 | tf_op jit(solution)/shard_map/all_gather | solution.py:61
  138.7 6.5 copy.16
  145.2 4.1 dynamic_update_slice.24
  149.4 3.2 copy-done
  152.6 3.1 fusion.15
  156.8 57.5 %all-reduce.9.cloned.1.call-done = bf16[4,128,128]{1,2,0:T(8,128)(2,1)} async-done(((bf16[4,128,128]{1,2,0:T(8,128)(2,1)}), bf16[4,128,128]{1,2,0:T(8,128)(2,1)}) %all-reduce.9.cloned.1.call-update) | async-done | bytes 131088 | tf_op jit(solution)/shard_map/psum | solution.py:56
  214.3 1.8 fusion.17
  216.2 46.9 %all-gather.22.cloned.1.call-done = bf16[4,2048,128]{1,2,0:T(8,128)(2,1)} async-done(((bf16[4,128,128]{1,2,0:T(8,128)(2,1)}), bf16[4,2048,128]{1,2,0:T(8,128)(2,1)}) %all-gather.22.cloned.1.call-update) | async-done | bytes 2097168 | tf_op jit(solution)/shard_map/all_gather | solution.py:61
  263.0 3.0 copy.18
  266.1 1.4 constant_dynamic-update-slice_fusion.5
  267.5 3.0 fusion.22
  271.7 57.5 %all-reduce.11.cloned.1.call-done = bf16[2,128,128]{1,2,0:T(8,128)(2,1)} async-done(((bf16[2,128,128]{1,2,0:T(8,128)(2,1)}), bf16[2,128,128]{1,2,0:T(8,128)(2,1)}) %all-reduce.11.cloned.1.call-update) | async-done | bytes 65552 | tf_op jit(solution)/shard_map/psum | solution.py:56
  329.2 1.6 fusion.23
  330.9 43.1 %all-gather.24.cloned.1.call-done = bf16[2,2048,128]{1,2,0:T(8,128)(2,1)} async-done(((bf16[2,128,128]{1,2,0:T(8,128)(2,1)}), bf16[2,2048,128]{1,2,0:T(8,128)(2,1)}) %all-gather.24.cloned.1.call-update) | async-done | bytes 1048592 | tf_op jit(solution)/shard_map/all_gather | solution.py:61
  374.0 1.6 copy.20
  375.6 1.1 constant_dynamic-update-slice_fusion.4
  376.7 3.2 fusion.20
  380.1 58.3 %all-reduce.13.cloned.1.call-done = bf16[2,128,128]{1,2,0:T(8,128)(2,1)} async-done(((bf16[2,128,128]{1,2,0:T(8,128)(2,1)}), bf16[2,128,128]{1,2,0:T(8,128)(2,1)}) %all-reduce.13.cloned.1.call-update) | async-done | bytes 65552 | tf_op jit(solution)/shard_map/psum | solution.py:56
  438.4 1.6 fusion.24
  440.1 43.3 %all-gather.26.cloned.1.call-done = bf16[2,2048,128]{1,2,0:T(8,128)(2,1)} async-done(((bf16[2,128,128]{1,2,0:T(8,128)(2,1)}), bf16[2,2048,128]{1,2,0:T(8,128)(2,1)}) %all-gather.26.cloned.1.call-update) | async-done | bytes 1048592 | tf_op jit(solution)/shard_map/all_gather | solution.py:61
  483.4 1.6 copy.22
  485.0 1.1 constant_dynamic-update-slice_fusion.3
  486.1 1.7 fusion.25
  488.0 42.5 %all-gather.28.cloned.1.call-done = bf16[2,2048,128]{1,2,0:T(8,128)(2,1)} async-done(((bf16[2,128,128]{1,2,0:T(8,128)(2,1)}), bf16[2,2048,128]{1,2,0:T(8,128)(2,1)}) %all-gather.28.cloned.1.call-update) | async-done | bytes 1048592 | tf_op jit(solution)/shard_map/all_gather | solution.py:61
  530.4 1.6 copy.25
  532.1 5.3 dynamic_update_slice.28
  537.4 1.9 fusion.21
  540.4 57.5 %all-reduce.15.cloned.1.call-done = bf16[2,128,128]{1,2,0:T(8,128)(2,1)} async-done(((bf16[2,128,128]{1,2,0:T(8,128)(2,1)}), bf16[2,128,128]{1,2,0:T(8,128)(2,1)}) %all-reduce.15.cloned.1.call-update) | async-done | bytes 65552 | tf_op jit(solution)/shard_map/psum | solution.py:56
  597.8 1.6 fusion.26
  599.7 43.1 %all-gather.30.cloned.1.call-done = bf16[2,2048,128]{1,2,0:T(8,128)(2,1)} async-done(((bf16[2,128,128]{1,2,0:T(8,128)(2,1)}), bf16[2,2048,128]{1,2,0:T(8,128)(2,1)}) %all-gather.30.cloned.1.call-update) | async-done | bytes 1048592 | tf_op jit(solution)/shard_map/all_gather | solution.py:61
  642.8 1.6 copy.27
  644.4 1.0 constant_dynamic-update-slice_fusion.2
  645.5 2.5 fusion.14
  649.1 57.6 %all-reduce.17.cloned.1.call-done = bf16[4,128,128]{1,2,0:T(8,128)(2,1)} async-done(((bf16[4,128,128]{1,2,0:T(8,128)(2,1)}), bf16[4,128,128]{1,2,0:T(8,128)(2,1)}) %all-reduce.17.cloned.1.call-update) | async-done | bytes 131088 | tf_op jit(solution)/shard_map/psum | solution.py:56
  706.7 1.8 fusion.18
  708.6 47.0 %all-gather.32.cloned.1.call-done = bf16[4,2048,128]{1,2,0:T(8,128)(2,1)} async-done(((bf16[4,128,128]{1,2,0:T(8,128)(2,1)}), bf16[4,2048,128]{1,2,0:T(8,128)(2,1)}) %all-gather.32.cloned.1.call-update) | async-done | bytes 2097168 | tf_op jit(solution)/shard_map/all_gather | solution.py:61
  755.6 3.0 copy.29
  758.6 1.5 constant_dynamic-update-slice_fusion.1
  760.1 4.6 fusion.10
  764.8 1.0 constant_dynamic-slice_fusion.5
  765.9 58.0 %all-reduce.19.cloned.1.call-done = bf16[8,128,128]{1,2,0:T(8,128)(2,1)} async-done(((bf16[8,128,128]{1,2,0:T(8,128)(2,1)}), bf16[8,128,128]{1,2,0:T(8,128)(2,1)}) %all-reduce.19.cloned.1.call-update) | async-done | bytes 262160 | tf_op jit(solution)/shard_map/psum | solution.py:56
  823.9 2.0 fusion.12
  825.9 56.9 %all-gather.34.cloned.1.call-done = bf16[8,2048,128]{1,2,0:T(8,128)(2,1)} async-done(((bf16[8,128,128]{1,2,0:T(8,128)(2,1)}), bf16[8,2048,128]{1,2,0:T(8,128)(2,1)}) %all-gather.34.cloned.1.call-update) | async-done | bytes 4194320 | tf_op jit(solution)/shard_map/all_gather | solution.py:61
  882.9 6.5 copy.31
  889.4 4.7 constant_dynamic-update-slice_fusion
  894.1 1.5 constant_dynamic-slice_fusion.4
  (59 shorter events, 7.1 us)
Async XLA Ops:
  6.5 77.3 %all-gather.18.cloned.1.call-start = ((), (), s32[]{:S(2)}) async-start(), calls=%async_computation | async-start | bytes 8454144 | tf_op jit(solution)/shard_map/all_gather | solution.py:79
  7.3 131.5 %all-gather.20.cloned.1.call-start = ((), (), s32[]{:S(2)}) async-start(), calls=%async_computation.7 | async-start | bytes 4456448 | tf_op jit(solution)/shard_map/all_gather | solution.py:61
  85.9 128.4 %all-reduce.9.cloned.1.call-start = ((), (), s32[]{:S(2)}) async-start(), calls=%async_computation.1 | async-start | bytes 262144 | tf_op jit(solution)/shard_map/psum | solution.py:56
  145.2 69.1 %copy-start.1 = (bf16[16,1,128,128]{3,2,1,0:T(8,128)(2,1)S(1)}, bf16[16,1,128,128]{3,2,1,0:T(8,128)(2,1)}, u32[]{:S(2)}) copy-start(bf16[16,1,128,128]{3,2,1,0:T(8,128)(2,1)} %param.8) | copy-start | bytes 1572868
  145.2 70.9 %copy-start.3 = (s32[16,1,32,1]{2,3,1,0:T(1,128)S(1)}, s32[16,1,32,1]{2,3,1,0:T(1,128)}, u32[]{:S(2)}) copy-start(s32[16,1,32,1]{2,3,1,0:T(1,128)} %param.7) | copy-start | bytes 6148
  149.3 3.2 copy-start
  155.7 107.3 %all-gather.22.cloned.1.call-start = ((), (), s32[]{:S(2)}) async-start(), calls=%async_computation.8 | async-start | bytes 2228224 | tf_op jit(solution)/shard_map/all_gather | solution.py:61
  216.1 113.1 %all-reduce.11.cloned.1.call-start = ((), (), s32[]{:S(2)}) async-start(), calls=%async_computation.2 | async-start | bytes 131072 | tf_op jit(solution)/shard_map/psum | solution.py:56
  267.5 218.5 %copy-start.2 = (bf16[16,1,128,128]{3,2,1,0:T(8,128)(2,1)S(1)}, bf16[16,1,128,128]{3,2,1,0:T(8,128)(2,1)}, u32[]{:S(2)}) copy-start(bf16[16,1,128,128]{3,2,1,0:T(8,128)(2,1)} %param.9) | copy-start | bytes 1572868
  270.6 103.4 %all-gather.24.cloned.1.call-start = ((), (), s32[]{:S(2)}) async-start(), calls=%async_computation.9 | async-start | bytes 1114112 | tf_op jit(solution)/shard_map/all_gather | solution.py:61
  330.8 107.6 %all-reduce.13.cloned.1.call-start = ((), (), s32[]{:S(2)}) async-start(), calls=%async_computation.3 | async-start | bytes 131072 | tf_op jit(solution)/shard_map/psum | solution.py:56
  379.9 103.5 %all-gather.26.cloned.1.call-start = ((), (), s32[]{:S(2)}) async-start(), calls=%async_computation.10 | async-start | bytes 1114112 | tf_op jit(solution)/shard_map/all_gather | solution.py:61
  440.1 90.4 %all-gather.28.cloned.1.call-start = ((), (), s32[]{:S(2)}) async-start(), calls=%async_computation.11 | async-start | bytes 1114112 | tf_op jit(solution)/shard_map/all_gather | solution.py:61
  487.8 110.1 %all-reduce.15.cloned.1.call-start = ((), (), s32[]{:S(2)}) async-start(), calls=%async_computation.4 | async-start | bytes 131072 | tf_op jit(solution)/shard_map/psum | solution.py:56
  539.3 103.5 %all-gather.30.cloned.1.call-start = ((), (), s32[]{:S(2)}) async-start(), calls=%async_computation.12 | async-start | bytes 1114112 | tf_op jit(solution)/shard_map/all_gather | solution.py:61
  599.5 107.2 %all-reduce.17.cloned.1.call-start = ((), (), s32[]{:S(2)}) async-start(), calls=%async_computation.5 | async-start | bytes 262144 | tf_op jit(solution)/shard_map/psum | solution.py:56
  648.0 107.6 %all-gather.32.cloned.1.call-start = ((), (), s32[]{:S(2)}) async-start(), calls=%async_computation.13 | async-start | bytes 2228224 | tf_op jit(solution)/shard_map/all_gather | solution.py:61
  708.5 115.5 %all-reduce.19.cloned.1.call-start = ((), (), s32[]{:S(2)}) async-start(), calls=%async_computation.6 | async-start | bytes 524288 | tf_op jit(solution)/shard_map/psum | solution.py:56
  764.7 118.2 %all-gather.34.cloned.1.call-start = ((), (), s32[]{:S(2)}) async-start(), calls=%async_computation.14 | async-start | bytes 4456448 | tf_op jit(solution)/shard_map/all_gather | solution.py:61
Sparse Core Ops, SparseCore 0:
  10.5 73.2 all-gather.17
  86.0 52.6 all-gather.19
  155.9 58.4 all-reduce.8
  216.3 46.7 all-gather.21
  270.7 58.4 all-reduce.10
  331.1 42.8 all-gather.23
  380.0 58.3 all-reduce.12
  440.5 42.8 all-gather.25
  487.9 42.5 all-gather.27
  539.4 58.3 all-reduce.14
  600.0 42.8 all-gather.29
  648.1 58.5 all-reduce.16
  708.8 46.7 all-gather.31
  764.8 59.0 all-reduce.18
  826.1 56.7 all-gather.33
where the time goes:
time: 904 us; the launch traced here: 902 us
  waiting for transfers between devices  799 us (88%)
  local copies, waits for them, and re-layouts  55.9 us (6%)
  matrix products  32.5 us (4%)
  between operations  13.5 us (1%)
    all_gather x8, waiting for transfers between devices, finish_level(): gathered = lax.all_gather(solved[:, None], 'pcol', axis=1, tiled=True)  375 us
    psum x6, waiting for transfers between devices, finish_level(): lax.psum(partial_value.astype(jnp.bfloat16), 'prow').astype(jnp.float32)  346 us
    all_gather x1, waiting for transfers between devices, on_device(): lax.all_gather(right_sides, ('prow', 'pcol'), axis=0, tiled=True)  76.5 us
    all_gather x8, local copies, waits for them, and re-layouts, finish_level(): gathered = lax.all_gather(solved[:, None], 'pcol', axis=1, tiled=True)  25.4 us
    dot_general x6, matrix products, level_sums(): jnp.einsum('ijab,jbn->ian', masked, column_vals, preferred_element_type=j...  18.3 us
  transfers between devices with their start and end apart: 15, of which 15 were waited for; matrix products, arithmetic and copies ran while one was open for 1% of the time, Pallas kernels for 0%

commit v1 on v0

v1 whole, which is shorter than its diff:
```python
import jax
import jax.numpy as jnp
from jax import lax
from jax.experimental import pallas as pl
from jax.experimental.pallas import tpu as pltpu
from jax.sharding import PartitionSpec as P

MESH = pl.DeviceIdType.MESH
S = 128
BF = jnp.bfloat16
F32 = jnp.float32
NP, NQ = 8, 16

GROUPS = ((8, 16, 0, 16), (12, 16, 16, 24), (14, 16, 24, 28), (12, 14, 28, 32), (8, 12, 24, 32), (0, 8, 16, 32))


def nt(a, b):
    return lax.dot_general(a, b, (((1,), (1,)), ((), ())), preferred_element_type=F32)


def level0_row(p):
    y = p // 2
    return 2 * ((2 * y - y // 2) % 4) + p % 2


def kernel(
    rhs_hbm, factor_hbm, pattern, lower_hbm, upper_hbm, out_ref,
    raw, fm, yt, xt, rhs_v, rhs_t, b0, b1, b2, b3, linv0, linv, uinv,
    ps1, ps2, ps3, ps0, rb1, rb2, rb3, rbb2, rbb1, rb0, psb2, psb1,
    y0s, y1s, y2s, y3s, x3s, x2s, x1s, x0s, y0own, xo, accf, acc1, acc0,
    lsem, gsem, bsem, osem, rs_s, rs_r, mc_s, mc_s0, mc_r, l0_s, l0_r, b_s, b_r, yo_s, yo_r, xo_s, xo_r,
):
    p = lax.axis_index("prow")
    q = lax.axis_index("pcol")
    me = p * NQ + q

    load_rhs = pltpu.make_async_copy(rhs_hbm, rhs_v, lsem)
    load_rhs.start()
    loads = []
    for g, (r0, r1, c0, c1) in enumerate(GROUPS):
        c = pltpu.make_async_copy(
            factor_hbm.at[r0:r1, c0:c1], raw.at[r0:r1, c0:c1], gsem.at[g]
        )
        c.start()
        loads.append(c)
    row1, row2, row3, row0 = 8 + p // 2, 12 + p // 4, 14 + p // 4, level0_row(p)
    inv_loads = []
    for k, r in enumerate((row1, row2, row3)):
        inv_loads.append(pltpu.make_async_copy(lower_hbm.at[r], linv.at[k], bsem.at[k]))
    for k, r in enumerate((row1, row2, row3, row0)):
        inv_loads.append(pltpu.make_async_copy(upper_hbm.at[r], uinv.at[k], bsem.at[3 + k]))
    for c in inv_loads:
        c.start()

    barrier = pltpu.get_barrier_semaphore()

    def greet(k, carry):
        o = (me + k) % (NP * NQ)
        pl.semaphore_signal(barrier, 1, device_id=(o // NQ, o % NQ), device_id_type=MESH)
        return carry

    lax.fori_loop(1, NP * NQ, greet, 0)

    load_rhs.wait()
    for s in range(2):
        rhs_t[s] = rhs_v[s * S:(s + 1) * S, :].astype(F32).T.astype(BF)

    pl.semaphore_wait(barrier, NP * NQ - 1)

    def send(src, dst, ssem, rsem, dp, dq):
        here = (dp == p) & (dq == q)
        remote = pltpu.make_async_remote_copy(
            src_ref=src, dst_ref=dst, send_sem=ssem, recv_sem=rsem, device_id=(dp, dq), device_id_type=MESH
        )

        @pl.when(here)
        def _():
            pltpu.make_async_copy(src, dst, rsem).start()

        @pl.when(jnp.logical_not(here))
        def _():
            remote.start()

        def finish():
            @pl.when(jnp.logical_not(here))
            def _():
                remote.wait_send()

        return finish

    def arrived(ref, sem):
        pltpu.make_async_copy(ref, ref, sem).wait()

    def level0_q(jb):
        return (jb % 4) * 4 + jb // 4

    owner = q % NP == p

    @pl.when(owner)
    def _():
        for r in range(8):
            send(lower_hbm.at[r], linv0, l0_s.at[r], l0_r, p, level0_q(2 * r + q // 8))

    @pl.when(p < 4)
    def _():
        for s in range(2):
            n = 2 * me + s
            send(rhs_t.at[s], b0, b_s.at[s], b_r.at[0], n % 8, level0_q(n // 8))

    @pl.when((p >= 4) & (p < 6))
    def _():
        for s in range(2):
            n = 2 * me + s
            for h in range(2):
                send(rhs_t.at[s, pl.ds(64 * h, 64)], b1, b_s.at[2 * s + h], b_r.at[1], 2 * (n // 16 - 8) + h, n % 16)

    for lev, (at_p, dst) in enumerate(((6, b2), (7, b3))):
        @pl.when(p == at_p)
        def _():
            for s in range(2):
                n = 2 * me + s
                for c in range(4):
                    send(
                        rhs_t.at[s, pl.ds(32 * c, 32)], dst, b_s.at[4 * s + c], b_r.at[2 + lev],
                        4 * (n // 16 - 12 - 2 * lev) + c, n % 16,
                    )

    def mask_group(g):
        r0, r1, c0, c1 = GROUPS[g]
        loads[g].wait()

        def row(i, carry):
            for j in range(c0, c1):
                keep = jnp.where(pattern[i, j] > 0, 1.0, 0.0).astype(F32)
                m = jnp.full((S, S), keep, F32).astype(BF)
                fm[pl.ds(pl.multiple_of(i * S, S), S), j * S:(j + 1) * S] = raw[i, j] * m
            return carry

        lax.fori_loop(r0, r1, row, 0)

    mask_group(0)

    def multicast(idx, stage, buf, col, n0, rows, tp):
        dst = buf.at[pl.ds(n0, rows), pl.ds(pl.multiple_of(col * S, S), S)]
        first = send(stage, dst, mc_s0.at[idx], mc_r.at[idx], tp, q)

        def one(k, carry):
            pltpu.make_async_remote_copy(
                src_ref=stage, dst_ref=dst, send_sem=mc_s.at[idx], recv_sem=mc_r.at[idx],
                device_id=(tp, (q + k) % NQ), device_id_type=MESH,
            ).start()
            return carry

        lax.fori_loop(1, NQ, one, 0)

        def finish():
            first()
            ref = fm.at[0:(NQ - 1) * rows, 0:S]
            arrived(ref, mc_s.at[idx])

        return finish

    def exchange(idx, ps, rb):
        for k in range(1, NP):
            d = (p + k) % NP
            pltpu.make_async_remote_copy(
                src_ref=ps.at[d], dst_ref=rb.at[k - 1], send_sem=rs_s.at[idx], recv_sem=rs_r.at[idx],
                device_id=(d, q), device_id_type=MESH,
            ).start()

        def finish():
            arrived(rb, rs_s.at[idx])

        return finish

    def summed(idx, ps, rb):
        arrived(rb, rs_r.at[idx])
        total = ps[p].astype(F32)
        for k in range(NP - 1):
            total = total + rb[k].astype(F32)
        return total

    def split(part, ps, per_row, rows):
        for d in range(NP):
            r, c = d // per_row, d % per_row
            ps[d] = part[c * rows:(c + 1) * rows, r * S:(r + 1) * S].astype(BF)

    tp = q % NP
    hi = q // NP
    done = []

    arrived(b0, b_r.at[0])
    arrived(linv0, l0_r)
    y0s[...] = nt(b0[...], linv0[...]).astype(BF)
    done.append(multicast(0, y0s, yt, (q % 4) * 4 + q // 4, 0, S, p))
    mask_group(1)
    mask_group(2)
    arrived(yt.at[:, 0:16 * S], mc_r.at[0])

    split(nt(yt[:, 0:16 * S], fm[8 * S:12 * S, 0:16 * S]), ps1, 2, 64)
    done.append(exchange(0, ps1, rb1))

    @pl.when(owner)
    def _():
        for d in range(NP):
            col = 2 * level0_row(d) + hi
            send(yt.at[:, pl.ds(pl.multiple_of(col * S, S), S)], y0own, yo_s.at[d], yo_r, d, q)

    accf[...] = nt(yt[:, 0:16 * S], fm[12 * S:16 * S, 0:16 * S])
    for c in inv_loads:
        c.wait()
    arrived(b1, b_r.at[1])
    e = (b1[...].astype(F32) - summed(0, ps1, rb1)).astype(BF)
    y1s[...] = nt(e, linv[0]).astype(BF)
    n1 = pl.multiple_of((p % 2) * 64, 64)
    n2 = pl.multiple_of((p % 4) * 32, 32)
    done.append(multicast(1, y1s, yt, 2 * row1 + hi, n1, 64, tp))
    for g in (3, 4, 5):
        mask_group(g)
    arrived(yt.at[:, 16 * S:24 * S], mc_r.at[1])

    split(accf[:, 0:2 * S] + nt(yt[:, 16 * S:24 * S], fm[12 * S:14 * S, 16 * S:24 * S]), ps2, 4, 32)
    done.append(exchange(1, ps2, rb2))
    accf[:, 2 * S:4 * S] += nt(yt[:, 16 * S:24 * S], fm[14 * S:16 * S, 16 * S:24 * S])
    arrived(b2, b_r.at[2])
    e = (b2[...].astype(F32) - summed(1, ps2, rb2)).astype(BF)
    y2s[...] = nt(e, linv[1]).astype(BF)
    done.append(multicast(2, y2s, yt, 2 * row2 + hi, n2, 32, tp))
    arrived(yt.at[:, 24 * S:28 * S], mc_r.at[2])

    split(accf[:, 2 * S:4 * S] + nt(yt[:, 24 * S:28 * S], fm[14 * S:16 * S, 24 * S:28 * S]), ps3, 4, 32)
    done.append(exchange(2, ps3, rb3))
    arrived(b3, b_r.at[3])
    e = (b3[...].astype(F32) - summed(2, ps3, rb3)).astype(BF)
    y3s[...] = nt(e, linv[2]).astype(BF)
    x3s[...] = nt(y3s[...], uinv[2]).astype(BF)
    done.append(multicast(3, x3s, xt, 2 * row3 + hi - 16, n2, 32, tp))
    done.append(send(x3s, xo.at[q % 2, pl.ds(n2, 32)], xo_s.at[3], xo_r, 7, 8 * (row3 % 2) + q // 2))
    arrived(xt.at[:, 12 * S:16 * S], mc_r.at[3])

    split(nt(xt[:, 12 * S:16 * S], fm[12 * S:14 * S, 28 * S:32 * S]), psb2, 4, 32)
    done.append(exchange(3, psb2, rbb2))
    acc1[...] = nt(xt[:, 12 * S:16 * S], fm[8 * S:12 * S, 28 * S:32 * S])
    acc0[...] = nt(xt[:, 12 * S:16 * S], fm[0:8 * S, 28 * S:32 * S])
    g = (y2s[...].astype(F32) - summed(3, psb2, rbb2)).astype(BF)
    x2s[...] = nt(g, uinv[1]).astype(BF)
    done.append(multicast(4, x2s, xt, 2 * row2 + hi - 16, n2, 32, tp))
    done.append(send(x2s, xo.at[q % 2, pl.ds(n2, 32)], xo_s.at[2], xo_r, 6, 8 * (row2 % 2) + q // 2))
    arrived(xt.at[:, 8 * S:12 * S], mc_r.at[4])

    split(acc1[...] + nt(xt[:, 8 * S:12 * S], fm[8 * S:12 * S, 24 * S:28 * S]), psb1, 2, 64)
    done.append(exchange(4, psb1, rbb1))
    acc0[...] += nt(xt[:, 8 * S:12 * S], fm[0:8 * S, 24 * S:28 * S])
    g = (y1s[...].astype(F32) - summed(4, psb1, rbb1)).astype(BF)
    x1s[...] = nt(g, uinv[0]).astype(BF)
    done.append(multicast(5, x1s, xt, 2 * row1 + hi - 16, n1, 64, tp))
    done.append(send(x1s, xo.at[q % 2, pl.ds(n1, 64)], xo_s.at[1], xo_r, row1 // 2, 8 * (row1 % 2) + q // 2))
    arrived(xt.at[:, 0:8 * S], mc_r.at[5])

    part = acc0[...] + nt(xt[:, 0:8 * S], fm[0:8 * S, 16 * S:24 * S])
    for d in range(NP):
        r = level0_row(d)
        ps0[d] = part[:, r * S:(r + 1) * S].astype(BF)
    done.append(exchange(5, ps0, rb0))
    arrived(y0own, yo_r)
    g = (y0own[...].astype(F32) - summed(5, ps0, rb0)).astype(BF)
    x0s[...] = nt(g, uinv[3]).astype(BF)
    done.append(send(x0s, xo.at[q % 2], xo_s.at[0], xo_r, row0 // 2, 8 * (row0 % 2) + q // 2))
    arrived(xo, xo_r)
    for s in range(2):
        out_ref[s * S:(s + 1) * S, :] = xo[s].astype(F32).T.astype(BF)

    for f in done:
        f()

    @pl.when(owner)
    def _():
        for r in range(8):
            dq = level0_q(2 * r + q // 8)

            @pl.when(dq != q)
            def _():
                arrived(linv0, l0_s.at[r])

        for d in range(NP):
            @pl.when(d != p)
            def _():
                arrived(y0own, yo_s.at[d])

    @pl.when(p < 4)
    def _():
        for s in range(2):
            n = 2 * me + s

            @pl.when(jnp.logical_not((n % 8 == p) & (level0_q(n // 8) == q)))
            def _():
                arrived(b0, b_s.at[s])

    @pl.when((p >= 4) & (p < 6))
    def _():
        for s in range(2):
            n = 2 * me + s
            for h in range(2):
                @pl.when(jnp.logical_not((2 * (n // 16 - 8) + h == p) & (n % 16 == q)))
                def _():
                    arrived(b1, b_s.at[2 * s + h])

    for lev, (at_p, dst) in enumerate(((6, b2), (7, b3))):
        @pl.when(p == at_p)
        def _():
            for s in range(2):
                n = 2 * me + s
                for c in range(4):
                    @pl.when(jnp.logical_not((4 * (n // 16 - 12 - 2 * lev) + c == p) & (n % 16 == q)))
                    def _():
                        arrived(dst, b_s.at[4 * s + c])


def on_device(right_sides, factor, pattern, lower_inverse, upper_inverse):
    vm = pltpu.VMEM
    dma = pltpu.SemaphoreType.DMA
    hbm = pl.BlockSpec(memory_space=pl.ANY)
    return pl.pallas_call(
        kernel,
        out_shape=jax.ShapeDtypeStruct(right_sides.shape, BF),
        in_specs=[hbm, hbm, pl.BlockSpec(memory_space=pltpu.SMEM), hbm, hbm],
        out_specs=pl.BlockSpec(memory_space=pltpu.VMEM),
        scratch_shapes=[
            vm((16, 32, S, S), BF), vm((16 * S, 32 * S), BF), vm((S, 28 * S), BF), vm((S, 16 * S), BF),
            vm((2 * S, S), BF), vm((2, S, S), BF),
            vm((S, S), BF), vm((64, S), BF), vm((32, S), BF), vm((32, S), BF),
            vm((S, S), BF), vm((3, S, S), BF), vm((4, S, S), BF),
            vm((8, 64, S), BF), vm((8, 32, S), BF), vm((8, 32, S), BF), vm((8, S, S), BF),
            vm((7, 64, S), BF), vm((7, 32, S), BF), vm((7, 32, S), BF), vm((7, 32, S), BF), vm((7, 64, S), BF),
            vm((7, S, S), BF), vm((8, 32, S), BF), vm((8, 64, S), BF),
            vm((S, S), BF), vm((64, S), BF), vm((32, S), BF), vm((32, S), BF),
            vm((32, S), BF), vm((32, S), BF), vm((64, S), BF), vm((S, S), BF),
            vm((S, S), BF), vm((2, S, S), BF),
            vm((S, 4 * S), F32), vm((S, 4 * S), F32), vm((S, 8 * S), F32),
            dma, dma((6,)), dma((7,)), dma, dma((6,)), dma((6,)), dma((6,)), dma((6,)), dma((6,)),
            dma((8,)), dma, dma((8,)), dma((4,)), dma((8,)), dma, dma((4,)), dma,
        ],
        compiler_params=pltpu.CompilerParams(
            collective_id=0, has_side_effects=True, vmem_limit_bytes=60 * 1024 * 1024
        ),
    )(
        right_sides,
        factor.reshape(16, 32, S, S),
        pattern.reshape(16, 32),
        lower_inverse.reshape(16, S, S),
        upper_inverse.reshape(16, S, S),
    )


def solution(mesh):
    return jax.shard_map(
        on_device,
        mesh=mesh,
        in_specs=(
            P(("prow", "pcol"), None),
            P(None, "pcol", None, "prow", None, None),
            P(None, "pcol", None, "prow"),
            P(None, "pcol", None, None),
            P(None, "pcol", None, None),
        ),
        out_specs=P(("prow", "pcol"), None),
        check_vma=False,
    )
```

time: 904 us -> 96.7 us (0.11)
  waiting for transfers between devices: 799 us -> 0 us
  Pallas kernels: 0 us -> 95 us
  local copies, waits for them, and re-layouts: 55.9 us -> 1.47 us
  matrix products: 32.5 us -> 0 us
  between operations: 13.5 us -> 0.01 us
    all_gather x9 -> x0, waiting for transfers between devices: 451 us -> none  [the longest x8 375 us: finish_level(): gathered = lax.all_gather(solved[:, None], 'pcol', axis=1, tiled=True)]
    psum x6 -> x0, waiting for transfers between devices: 346 us -> none  [finish_level(): lax.psum(partial_value.astype(jnp.bfloat16), 'prow').astype(jnp.float32)]
    pallas_call x0 -> x1, Pallas kernels: none -> 95 us  [on_device(): pl.pallas_call(kernel, out_shape=jax.ShapeDtypeStruct(right_sides.shape,...]
    dot_general x14 -> x0, matrix products: 32.5 us -> none  [the longest x6 18.3 us: level_sums(): jnp.einsum('ijab,jbn->ian', masked, column_vals, preferred_element_type=j...]
    all_gather x8 -> x0, local copies, waits for them, and re-layouts: 25.4 us -> none  [finish_level(): gathered = lax.all_gather(solved[:, None], 'pcol', axis=1, tiled=True)]
    dynamic_update_slice x8 -> x0, local copies, waits for them, and re-layouts: 20.3 us -> none  [the longest x4 12.6 us: on_device(): lax.dynamic_update_slice_in_dim(backward_vals, solved, row_start * pcol_n...]
  transfers between devices with their start and end apart: 15 -> 0, of which waited for: 15 -> 0; matrix products, arithmetic and copies ran while one was open for 1% -> 0% of each run, Pallas kernels for 0% -> 0%
where the time goes in v1:
time: 96.7 us; the launch traced here: 96.5 us
  Pallas kernels  95 us (98%)
  local copies, waits for them, and re-layouts  1.47 us (2%)
    pallas_call x1, Pallas kernels, on_device(): pl.pallas_call(kernel, out_shape=jax.ShapeDtypeStruct(right_sides.shape,...  95 us

profile of v1, /device:TPU:1, one launch (start us, length us, event | category | flops | bytes accessed | tf_op | source)
XLA Modules:
  0.0 96.5 jit_solution(4149546962654950660)
XLA Ops:
  0.0 95.0 %shard_map.55 = bf16[256,128]{1,0:T(8,128)(2,1)} custom-call(bf16[256,128]{1,0:T(8,128)(2,1)} %rhs_hbm.1, bf16[16,32,128,128]{3,2,1,0:T(8,128)(2,1)} %bitcast.4, s32[16,32]{1,0:T(8,128)} %bitcast.7, bf16[16,128,128]{2,1,0:T(8,128)(2,1)} %bitcast.5, bf16[16,128,128]{2,1,0:T(8,128)(2,1)} %bitcast.6), custom_call_target="tpu_custom_call" | custom-call | tf_op jit(solution)/shard_map/pallas_call | solution.py:323
  95.0 1.5 %copy.7 = bf16[256,128]{1,0:T(8,128)(2,1)} copy(bf16[256,128]{1,0:T(8,128)(2,1)} %shard_map.55) | data formatting | bytes 131072

commit v2 on v1

v2 whole, which is shorter than its diff:
```python
import jax
import jax.numpy as jnp
from jax import lax
from jax.experimental import pallas as pl
from jax.experimental.pallas import tpu as pltpu
from jax.sharding import PartitionSpec as P

MESH = pl.DeviceIdType.MESH
S = 128
H = 64
BF = jnp.bfloat16
F32 = jnp.float32
NP, NQ = 8, 16

GROUPS = ((8, 16, 0, 16), (12, 16, 16, 24), (14, 16, 24, 28), (12, 14, 28, 32), (8, 12, 24, 32), (0, 8, 16, 32))
STEPS = sorted(
    ((dx, dz) for dx in range(4) for dz in range(4) if dx or dz),
    key=lambda s: -(min(s[0], 4 - s[0]) + min(s[1], 4 - s[1])),
)


def nt(a, b):
    return lax.dot_general(a, b, (((1,), (1,)), ((), ())), preferred_element_type=F32)


def level0_row(p):
    y = p // 2
    return 2 * ((2 * y - y // 2) % 4) + p % 2


def kernel(
    rhs_hbm, factor_hbm, pattern, lower_hbm, upper_hbm, out_ref,
    raw, fm, yt, xt, rhs_v, rhs_t, b0, bx, b1, b2, b3, linv0, linv, uinv,
    ps1, ps2, ps3, psb2, psb1, ps0, rb1, rb2, rb3, rbb2, rbb1, rb0,
    y0s, y1s, y2s, y3s, x3s, x2s, x1s, x0s, y0own, xo, accf, acc1, acc0,
    lsem, gsem, isem, rs_s, rs_r, mc_s, mc_s0, mc_r, l0_s, l0_r, b_s, b0_r, bx_r, bl_s, bl_r, yo_s, yo_r, xo_s, xo_r,
):
    p = lax.axis_index("prow")
    q = lax.axis_index("pcol")
    x, z = q // 4, q % 4
    me = p * NQ + q
    row1, row2, row3, row0 = 8 + p // 2, 12 + p // 4, 14 + p // 4, level0_row(p)

    barrier = pltpu.get_barrier_semaphore()

    def greet(dp, dq):
        pl.semaphore_signal(barrier, 1, device_id=(dp, dq), device_id_type=MESH)

    for dx, dz in STEPS:
        greet(p, (x + dx) % 4 * 4 + (z + dz) % 4)
    for k in range(1, NP):
        greet((p + k) % NP, q)
    corner = (p == 0) & (z == 0)

    @pl.when(jnp.logical_not(corner))
    def _():
        greet(z, x * 4 + p // 2)

    load_rhs = pltpu.make_async_copy(rhs_hbm, rhs_v, lsem)
    load_rhs.start()
    loads = []
    for g, (r0, r1, c0, c1) in enumerate(GROUPS):
        c = pltpu.make_async_copy(factor_hbm.at[r0:r1, c0:c1], raw.at[r0:r1, c0:c1], gsem.at[g])
        c.start()
        loads.append(c)
    inv_loads = []
    for k, r in enumerate((row1, row2, row3)):
        inv_loads.append(pltpu.make_async_copy(lower_hbm.at[r], linv.at[k], isem.at[k]))
    for k, r in enumerate((row1, row2, row3, row0)):
        inv_loads.append(pltpu.make_async_copy(upper_hbm.at[r], uinv.at[k], isem.at[3 + k]))
    for c in inv_loads:
        c.start()

    load_rhs.wait()
    for s in range(2):
        rhs_t[s] = rhs_v[s * S:(s + 1) * S, :].astype(F32).T.astype(BF)

    pl.semaphore_wait(
        barrier, 22 + jnp.where(p < 4, 2, 0) - jnp.where(corner, 1, 0)
    )

    def arrived(ref, sem):
        pltpu.make_async_copy(ref, ref, sem).wait()

    def send(src, dst, ssem, rsem, dp, dq):
        here = (dp == p) & (dq == q)

        @pl.when(here)
        def _():
            pltpu.make_async_copy(src, dst, rsem).start()

        @pl.when(jnp.logical_not(here))
        def _():
            pltpu.make_async_remote_copy(
                src_ref=src, dst_ref=dst, send_sem=ssem, recv_sem=rsem, device_id=(dp, dq), device_id_type=MESH
            ).start()

        def finish():
            @pl.when(jnp.logical_not(here))
            def _():
                arrived(src, ssem)

        return finish

    tp, hi = q % NP, q // NP
    owner = tp == p

    def level0_q(jb):
        return (jb % 4) * 4 + jb // 4

    @pl.when(owner)
    def _():
        for r in range(8):
            send(lower_hbm.at[r], linv0, l0_s.at[r], l0_r, p, level0_q(2 * r + hi))

    for s in range(2):
        @pl.when(p < 4)
        def _():
            send(rhs_t.at[s], b0, b_s.at[s], b0_r, 2 * z + s, x * 4 + p)

        @pl.when(p >= 4)
        def _():
            send(rhs_t.at[s], bx.at[hi], b_s.at[s], bx_r, p, 2 * tp + s)

    def spread_rhs(finish):
        for at, count, dst, sem in ((4, 2, b1, 0), (5, 2, b1, 0), (6, 4, b2, 1), (7, 4, b3, 2)):
            @pl.when(p == at)
            def _():
                for slot in range(2):
                    r = 2 * at + slot - (8, 12, 14)[sem]
                    rows = H // count
                    for c in range(count):
                        for h in range(2):
                            src = bx.at[slot, pl.ds(h * H + c * rows, rows)]
                            d = count * r + c
                            ssem = bl_s.at[(slot * count + c) * 2 + h]
                            if finish:
                                @pl.when(p != d)
                                def _():
                                    arrived(src, ssem)
                            else:
                                send(src, dst.at[h], ssem, bl_r.at[sem], d, q)

    def mask_group(g):
        r0, r1, c0, c1 = GROUPS[g]
        loads[g].wait()

        def row(i, carry):
            for j in range(c0, c1):
                keep = jnp.where(pattern[i, j] > 0, 1.0, 0.0).astype(F32)
                m = jnp.full((S, S), keep, F32).astype(BF)
                fm[pl.ds(pl.multiple_of(i * S, S), S), j * S:(j + 1) * S] = raw[i, j] * m
            return carry

        lax.fori_loop(r0, r1, row, 0)

    mask_group(0)
    done = []

    def multicast(h, idx, stage, buf, col, n0, rows, to):
        dst = buf.at[h, pl.ds(n0, rows), pl.ds(pl.multiple_of(col * S, S), S)]
        for dx, dz in STEPS:
            pltpu.make_async_remote_copy(
                src_ref=stage, dst_ref=dst, send_sem=mc_s.at[h, idx], recv_sem=mc_r.at[h, idx],
                device_id=(to, (x + dx) % 4 * 4 + (z + dz) % 4), device_id_type=MESH,
            ).start()
        first = send(stage, dst, mc_s0.at[h, idx], mc_r.at[h, idx], to, q)

        def finish():
            first()
            arrived(fm.at[0:(NQ - 1) * rows, 0:S], mc_s.at[h, idx])

        done.append(finish)

    def exchange(h, idx, ps, rb):
        for k in (4, 5, 3, 2, 6, 7, 1):
            d = (p + k) % NP
            pltpu.make_async_remote_copy(
                src_ref=ps.at[h, d], dst_ref=rb.at[h, k - 1], send_sem=rs_s.at[h, idx], recv_sem=rs_r.at[h, idx],
                device_id=(d, q), device_id_type=MESH,
            ).start()
        done.append(lambda: arrived(rb.at[h], rs_s.at[h, idx]))

    def summed(h, idx, ps, rb):
        arrived(rb.at[h], rs_r.at[h, idx])
        total = ps[h, p].astype(F32)
        for k in range(NP - 1):
            total = total + rb[h, k].astype(F32)
        return total

    def split(h, part, ps, per_row):
        rows = H // per_row
        for d in range(NP):
            r, c = d // per_row, d % per_row
            ps[h, d] = part[c * rows:(c + 1) * rows, r * S:(r + 1) * S].astype(BF)

    def cols(ref, h, c0, c1):
        return ref[h, :, c0 * S:c1 * S]

    def blocks(r0, r1, c0, c1):
        return fm[r0 * S:r1 * S, c0 * S:c1 * S]

    def to_output(h, lev, stage, slot_row, n0, rows):
        done.append(send(
            stage, xo.at[q % 2, pl.ds(h * H + n0, rows)], xo_s.at[h, lev], xo_r, slot_row // 2, 8 * (slot_row % 2) + q // 2
        ))

    n1 = pl.multiple_of((p % 2) * 32, 32)
    n2 = pl.multiple_of((p % 4) * 16, 16)

    def chain(h):
        lead = h == 0
        if lead:
            arrived(b0, b0_r)
            arrived(linv0, l0_r)
        y0s[h] = nt(b0[h * H:(h + 1) * H, :], linv0[...]).astype(BF)
        multicast(h, 0, y0s.at[h], yt, z * 4 + x, 0, H, p)
        yield
        if lead:
            @pl.when(p >= 4)
            def _():
                arrived(bx, bx_r)
            spread_rhs(False)
            mask_group(1)
            mask_group(2)
        arrived(yt.at[h, :, 0:16 * S], mc_r.at[h, 0])
        split(h, nt(cols(yt, h, 0, 16), blocks(8, 12, 0, 16)), ps1, 2)
        exchange(h, 0, ps1, rb1)
        yield
        @pl.when(owner)
        def _():
            for d in range(NP):
                col = 2 * level0_row(d) + hi
                send(yt.at[h, :, pl.ds(pl.multiple_of(col * S, S), S)], y0own.at[h], yo_s.at[h, d], yo_r.at[h], d, q)

        accf[h] = nt(cols(yt, h, 0, 16), blocks(12, 16, 0, 16))
        if lead:
            for c in inv_loads:
                c.wait()
            arrived(b1, bl_r.at[0])
        e = (b1[h].astype(F32) - summed(h, 0, ps1, rb1)).astype(BF)
        y1s[h] = nt(e, linv[0]).astype(BF)
        multicast(h, 1, y1s.at[h], yt, 2 * row1 + hi, n1, 32, tp)
        yield
        if lead:
            for g in (3, 4, 5):
                mask_group(g)
        arrived(yt.at[h, :, 16 * S:24 * S], mc_r.at[h, 1])
        split(h, accf[h, :, 0:2 * S] + nt(cols(yt, h, 16, 24), blocks(12, 14, 16, 24)), ps2, 4)
        exchange(h, 1, ps2, rb2)
        yield
        accf[h, :, 2 * S:4 * S] += nt(cols(yt, h, 16, 24), blocks(14, 16, 16, 24))
        if lead:
            arrived(b2, bl_r.at[1])
        e = (b2[h].astype(F32) - summed(h, 1, ps2, rb2)).astype(BF)
        y2s[h] = nt(e, linv[1]).astype(BF)
        multicast(h, 2, y2s.at[h], yt, 2 * row2 + hi, n2, 16, tp)
        yield
        arrived(yt.at[h, :, 24 * S:28 * S], mc_r.at[h, 2])
        split(h, accf[h, :, 2 * S:4 * S] + nt(cols(yt, h, 24, 28), blocks(14, 16, 24, 28)), ps3, 4)
        exchange(h, 2, ps3, rb3)
        yield
        if lead:
            arrived(b3, bl_r.at[2])
        e = (b3[h].astype(F32) - summed(h, 2, ps3, rb3)).astype(BF)
        y3s[h] = nt(e, linv[2]).astype(BF)
        x3s[h] = nt(y3s[h], uinv[2]).astype(BF)
        multicast(h, 3, x3s.at[h], xt, 2 * row3 + hi - 16, n2, 16, tp)
        to_output(h, 3, x3s.at[h], row3, n2, 16)
        yield
        arrived(xt.at[h, :, 12 * S:16 * S], mc_r.at[h, 3])
        split(h, nt(cols(xt, h, 12, 16), blocks(12, 14, 28, 32)), psb2, 4)
        exchange(h, 3, psb2, rbb2)
        yield
        acc1[h] = nt(cols(xt, h, 12, 16), blocks(8, 12, 28, 32))
        acc0[h] = nt(cols(xt, h, 12, 16), blocks(0, 8, 28, 32))
        g = (y2s[h].astype(F32) - summed(h, 3, psb2, rbb2)).astype(BF)
        x2s[h] = nt(g, uinv[1]).astype(BF)
        multicast(h, 4, x2s.at[h], xt, 2 * row2 + hi - 16, n2, 16, tp)
        to_output(h, 2, x2s.at[h], row2, n2, 16)
        yield
        arrived(xt.at[h, :, 8 * S:12 * S], mc_r.at[h, 4])
        split(h, acc1[h] + nt(cols(xt, h, 8, 12), blocks(8, 12, 24, 28)), psb1, 2)
        exchange(h, 4, psb1, rbb1)
        yield
        acc0[h] += nt(cols(xt, h, 8, 12), blocks(0, 8, 24, 28))
        g = (y1s[h].astype(F32) - summed(h, 4, psb1, rbb1)).astype(BF)
        x1s[h] = nt(g, uinv[0]).astype(BF)
        multicast(h, 5, x1s.at[h], xt, 2 * row1 + hi - 16, n1, 32, tp)
        to_output(h, 1, x1s.at[h], row1, n1, 32)
        yield
        arrived(xt.at[h, :, 0:8 * S], mc_r.at[h, 5])
        part = acc0[h] + nt(cols(xt, h, 0, 8), blocks(0, 8, 16, 24))
        for d in range(NP):
            r = level0_row(d)
            ps0[h, d] = part[:, r * S:(r + 1) * S].astype(BF)
        exchange(h, 5, ps0, rb0)
        yield
        arrived(y0own.at[h], yo_r.at[h])
        g = (y0own[h].astype(F32) - summed(h, 5, ps0, rb0)).astype(BF)
        x0s[h] = nt(g, uinv[3]).astype(BF)
        to_output(h, 0, x0s.at[h], row0, 0, H)
        yield

    chains = [chain(0), chain(1)]
    while chains:
        for c in list(chains):
            try:
                next(c)
            except StopIteration:
                chains.remove(c)

    arrived(xo, xo_r)
    for s in range(2):
        out_ref[s * S:(s + 1) * S, :] = xo[s].astype(F32).T.astype(BF)

    for f in done:
        f()

    @pl.when(owner)
    def _():
        for r in range(8):
            @pl.when(level0_q(2 * r + hi) != q)
            def _():
                arrived(linv0, l0_s.at[r])

        for d in range(NP):
            @pl.when(d != p)
            def _():
                for h in range(2):
                    arrived(y0own.at[h], yo_s.at[h, d])

    for s in range(2):
        @pl.when((p < 4) & jnp.logical_not((2 * z + s == p) & (p == z)))
        def _():
            arrived(b0, b_s.at[s])

        @pl.when((p >= 4) & (2 * tp + s != q))
        def _():
            arrived(b0, b_s.at[s])

    spread_rhs(True)


def on_device(right_sides, factor, pattern, lower_inverse, upper_inverse):
    def vm(*shape, dtype=BF):
        return pltpu.VMEM(shape, dtype)

    dma = pltpu.SemaphoreType.DMA
    hbm = pl.BlockSpec(memory_space=pl.ANY)
    return pl.pallas_call(
        kernel,
        out_shape=jax.ShapeDtypeStruct(right_sides.shape, BF),
        in_specs=[hbm, hbm, pl.BlockSpec(memory_space=pltpu.SMEM), hbm, hbm],
        out_specs=pl.BlockSpec(memory_space=pltpu.VMEM),
        scratch_shapes=[
            vm(16, 32, S, S), vm(16 * S, 32 * S), vm(2, H, 28 * S), vm(2, H, 16 * S),
            vm(2 * S, S), vm(2, S, S),
            vm(S, S), vm(2, S, S), vm(2, 32, S), vm(2, 16, S), vm(2, 16, S),
            vm(S, S), vm(3, S, S), vm(4, S, S),
            vm(2, 8, 32, S), vm(2, 8, 16, S), vm(2, 8, 16, S), vm(2, 8, 16, S), vm(2, 8, 32, S), vm(2, 8, H, S),
            vm(2, 7, 32, S), vm(2, 7, 16, S), vm(2, 7, 16, S), vm(2, 7, 16, S), vm(2, 7, 32, S), vm(2, 7, H, S),
            vm(2, H, S), vm(2, 32, S), vm(2, 16, S), vm(2, 16, S),
            vm(2, 16, S), vm(2, 16, S), vm(2, 32, S), vm(2, H, S),
            vm(2, H, S), vm(2, S, S),
            vm(2, H, 4 * S, dtype=F32), vm(2, H, 4 * S, dtype=F32), vm(2, H, 8 * S, dtype=F32),
            dma, dma((6,)), dma((7,)), dma((2, 6)), dma((2, 6)), dma((2, 6)), dma((2, 6)), dma((2, 6)),
            dma((8,)), dma, dma((2,)), dma, dma, dma((16,)), dma((3,)), dma((2, 8)), dma((2,)), dma((2, 4)), dma,
        ],
        compiler_params=pltpu.CompilerParams(
            collective_id=0, has_side_effects=True, vmem_limit_bytes=60 * 1024 * 1024
        ),
    )(
        right_sides,
        factor.reshape(16, 32, S, S),
        pattern.reshape(16, 32),
        lower_inverse.reshape(16, S, S),
        upper_inverse.reshape(16, S, S),
    )


def solution(mesh):
    return jax.shard_map(
        on_device,
        mesh=mesh,
        in_specs=(
            P(("prow", "pcol"), None),
            P(None, "pcol", None, "prow", None, None),
            P(None, "pcol", None, "prow"),
            P(None, "pcol", None, None),
            P(None, "pcol", None, None),
        ),
        out_specs=P(("prow", "pcol"), None),
        check_vma=False,
    )
```

time: 96.7 us -> 87.6 us (0.906)
  Pallas kernels: 95 us -> 86 us
    pallas_call x1, Pallas kernels: 95 us -> 86 us  [on_device(): pl.pallas_call(kernel, out_shape=jax.ShapeDtypeStruct(right_sides.shape,...]
where the time goes in v2:
time: 87.6 us; the launch traced here: 87.4 us
  Pallas kernels  86 us (98%)
  local copies, waits for them, and re-layouts  1.47 us (2%)
    pallas_call x1, Pallas kernels, on_device(): pl.pallas_call(kernel, out_shape=jax.ShapeDtypeStruct(right_sides.shape,...  86 us

profile of v2, /device:TPU:1, one launch (start us, length us, event | category | flops | bytes accessed | tf_op | source)
XLA Modules:
  0.0 87.4 jit_solution(12935163947400346389)
XLA Ops:
  0.0 86.0 %shard_map.55 = bf16[256,128]{1,0:T(8,128)(2,1)} custom-call(bf16[256,128]{1,0:T(8,128)(2,1)} %rhs_hbm.1, bf16[16,32,128,128]{3,2,1,0:T(8,128)(2,1)} %bitcast.4, s32[16,32]{1,0:T(8,128)} %bitcast.7, bf16[16,128,128]{2,1,0:T(8,128)(2,1)} %bitcast.5, bf16[16,128,128]{2,1,0:T(8,128)(2,1)} %bitcast.6), custom_call_target="tpu_custom_call" | custom-call | tf_op jit(solution)/shard_map/pallas_call | solution.py:351
  86.0 1.5 %copy.7 = bf16[256,128]{1,0:T(8,128)(2,1)} copy(bf16[256,128]{1,0:T(8,128)(2,1)} %shard_map.55) | data formatting | bytes 131072

commit v3 on v2

--- a/solution.py
+++ b/solution.py
@@ -12,7 +12,7 @@
 F32 = jnp.float32
 NP, NQ = 8, 16
 
-GROUPS = ((8, 16, 0, 16), (12, 16, 16, 24), (14, 16, 24, 28), (12, 14, 28, 32), (8, 12, 24, 32), (0, 8, 16, 32))
+GROUPS = ((14, 16, 24, 28), (8, 16, 0, 16), (12, 16, 16, 24), (12, 14, 28, 32), (8, 12, 24, 32), (0, 8, 16, 32))
 STEPS = sorted(
     ((dx, dz) for dx in range(4) for dz in range(4) if dx or dz),
     key=lambda s: -(min(s[0], 4 - s[0]) + min(s[1], 4 - s[1])),
@@ -31,15 +31,15 @@
 def kernel(
     rhs_hbm, factor_hbm, pattern, lower_hbm, upper_hbm, out_ref,
     raw, fm, yt, xt, rhs_v, rhs_t, b0, bx, b1, b2, b3, linv0, linv, uinv,
-    ps1, ps2, ps3, psb2, psb1, ps0, rb1, rb2, rb3, rbb2, rbb1, rb0,
+    ps1, ps2, ps3, psb1, ps0, rb1, rb2, rb3, rbb1, rb0, up, down, y2p, x3p,
     y0s, y1s, y2s, y3s, x3s, x2s, x1s, x0s, y0own, xo, accf, acc1, acc0,
-    lsem, gsem, isem, rs_s, rs_r, mc_s, mc_s0, mc_r, l0_s, l0_r, b_s, b0_r, bx_r, bl_s, bl_r, yo_s, yo_r, xo_s, xo_r,
+    lsem, gsem, isem, up_s, up_r, rs_s, rs_r, mc_s, mc_s0, mc_r, l0_s, l0_r, b_s, b0_r, bx_r, bl_s, bl_r, yo_s, yo_r, xo_s, xo_r,
 ):
     p = lax.axis_index("prow")
     q = lax.axis_index("pcol")
     x, z = q // 4, q % 4
     me = p * NQ + q
-    row1, row2, row3, row0 = 8 + p // 2, 12 + p // 4, 14 + p // 4, level0_row(p)
+    row1, row2, row3, row0 = 8 + p // 2, 12 + p % 2, 14 + p % 2, level0_row(p)
 
     barrier = pltpu.get_barrier_semaphore()
 
@@ -132,7 +132,7 @@
                     for c in range(count):
                         for h in range(2):
                             src = bx.at[slot, pl.ds(h * H + c * rows, rows)]
-                            d = count * r + c
+                            d = 2 * r + c if count == 2 else 2 * c + r
                             ssem = bl_s.at[(slot * count + c) * 2 + h]
                             if finish:
                                 @pl.when(p != d)
@@ -154,8 +154,48 @@
 
         lax.fori_loop(r0, r1, row, 0)
 
+    done = []
+
+    W = 4 * S
+    y = p // 2
+
+    def slabs(t, row, col, dst):
+        mine = pl.ds(pl.multiple_of(p * W, W), W)
+
+        def push(core, sem, dp, a0, a1):
+            pltpu.make_async_remote_copy(
+                src_ref=fm.at[pl.ds(pl.multiple_of((row + core) * S + a0, H), a1 - a0), col * S:col * S + W],
+                dst_ref=dst.at[a0:a1, mine],
+                send_sem=up_s.at[t], recv_sem=up_r.at[t, sem], device_id=(dp, q), device_id_type=MESH,
+            ).start()
+
+        for first in (True, False):
+            for core in (0, 1):
+                for sem, step in ((1, 1), (2, 3)):
+                    a0 = H * ((sem == 2) == first)
+                    push(core, sem if first else 0, (y + step) % 4 * 2 + core, a0, a0 + H)
+        push(1 - p % 2, 0, p + 1 - 2 * (p % 2), 0, S)
+        own = fm.at[pl.ds(pl.multiple_of((row + p % 2) * S, S), S), col * S:col * S + W]
+        pltpu.make_async_copy(own, dst.at[:, mine], up_r.at[t, 0]).start()
+        done.append(lambda: arrived(dst.at[:, 0:7 * W], up_s.at[t]))
+
+    def relay(t, dst):
+        for step, sem, a0 in ((1, 1, 0), (3, 2, H)):
+            lanes = pl.ds(pl.multiple_of((y + 4 - step) % 4 * 2 * W, 2 * W), 2 * W)
+            part = dst.at[a0:a0 + H, lanes]
+            arrived(part, up_r.at[t, sem])
+            pltpu.make_async_remote_copy(
+                src_ref=part, dst_ref=part, send_sem=up_s.at[t], recv_sem=up_r.at[t, 3],
+                device_id=((y + step) % 4 * 2 + p % 2, q), device_id_type=MESH,
+            ).start()
+
+    def whole(t, dst):
+        arrived(dst.at[:, 0:4 * W], up_r.at[t, 0])
+        arrived(dst.at[:, 0:2 * W], up_r.at[t, 3])
+
     mask_group(0)
-    done = []
+    slabs(0, 14, 24, up)
+    mask_group(1)
 
     def multicast(h, idx, stage, buf, col, n0, rows, to):
         dst = buf.at[h, pl.ds(n0, rows), pl.ds(pl.multiple_of(col * S, S), S)]
@@ -172,6 +212,19 @@
 
         done.append(finish)
 
+    def to_plane(h, idx, stage, buf):
+        col = tp * 4 + 2 * (p % 2) + hi
+        dst = buf.at[h, :, pl.ds(pl.multiple_of(col * S, S), S)]
+        for dx, dz in STEPS + [(0, 0)]:
+            for other in (0, 1):
+                if other or dx or dz:
+                    pltpu.make_async_remote_copy(
+                        src_ref=stage, dst_ref=dst, send_sem=mc_s.at[h, idx], recv_sem=mc_r.at[h, idx],
+                        device_id=(p + other * (1 - 2 * (p % 2)), (x + dx) % 4 * 4 + (z + dz) % 4), device_id_type=MESH,
+                    ).start()
+        pltpu.make_async_copy(stage, dst, mc_r.at[h, idx]).start()
+        done.append(lambda: arrived(fm.at[0:31 * 16, 0:S], mc_s.at[h, idx]))
+
     def exchange(h, idx, ps, rb):
         for k in (4, 5, 3, 2, 6, 7, 1):
             d = (p + k) % NP
@@ -191,7 +244,7 @@
     def split(h, part, ps, per_row):
         rows = H // per_row
         for d in range(NP):
-            r, c = d // per_row, d % per_row
+            r, c = (d // 2, d % 2) if per_row == 2 else (d % 2, d // 2)
             ps[h, d] = part[c * rows:(c + 1) * rows, r * S:(r + 1) * S].astype(BF)
 
     def cols(ref, h, c0, c1):
@@ -206,7 +259,7 @@
         ))
 
     n1 = pl.multiple_of((p % 2) * 32, 32)
-    n2 = pl.multiple_of((p % 4) * 16, 16)
+    n2 = pl.multiple_of((p // 2) * 16, 16)
 
     def chain(h):
         lead = h == 0
@@ -221,8 +274,9 @@
             def _():
                 arrived(bx, bx_r)
             spread_rhs(False)
-            mask_group(1)
+            relay(0, up)
             mask_group(2)
+            mask_group(3)
         arrived(yt.at[h, :, 0:16 * S], mc_r.at[h, 0])
         split(h, nt(cols(yt, h, 0, 16), blocks(8, 12, 0, 16)), ps1, 2)
         exchange(h, 0, ps1, rb1)
@@ -243,48 +297,52 @@
         multicast(h, 1, y1s.at[h], yt, 2 * row1 + hi, n1, 32, tp)
         yield
         if lead:
-            for g in (3, 4, 5):
+            for g in (4, 5):
                 mask_group(g)
         arrived(yt.at[h, :, 16 * S:24 * S], mc_r.at[h, 1])
         split(h, accf[h, :, 0:2 * S] + nt(cols(yt, h, 16, 24), blocks(12, 14, 16, 24)), ps2, 4)
         exchange(h, 1, ps2, rb2)
-        yield
-        accf[h, :, 2 * S:4 * S] += nt(cols(yt, h, 16, 24), blocks(14, 16, 16, 24))
+        split(h, accf[h, :, 2 * S:4 * S] + nt(cols(yt, h, 16, 24), blocks(14, 16, 16, 24)), ps3, 4)
+        exchange(h, 2, ps3, rb3)
+        yield
         if lead:
             arrived(b2, bl_r.at[1])
         e = (b2[h].astype(F32) - summed(h, 1, ps2, rb2)).astype(BF)
         y2s[h] = nt(e, linv[1]).astype(BF)
-        multicast(h, 2, y2s.at[h], yt, 2 * row2 + hi, n2, 16, tp)
-        yield
-        arrived(yt.at[h, :, 24 * S:28 * S], mc_r.at[h, 2])
-        split(h, accf[h, :, 2 * S:4 * S] + nt(cols(yt, h, 24, 28), blocks(14, 16, 24, 28)), ps3, 4)
-        exchange(h, 2, ps3, rb3)
-        yield
-        if lead:
+        to_plane(h, 2, y2s.at[h], y2p)
+        if lead:
+            slabs(1, 12, 28, down)
             arrived(b3, bl_r.at[2])
-        e = (b3[h].astype(F32) - summed(h, 2, ps3, rb3)).astype(BF)
+        rest = b3[h].astype(F32) - summed(h, 2, ps3, rb3)
+        yield
+        if lead:
+            relay(1, down)
+            whole(0, up)
+        arrived(y2p.at[h], mc_r.at[h, 2])
+        e = (rest - nt(y2p[h], up[...])).astype(BF)
         y3s[h] = nt(e, linv[2]).astype(BF)
         x3s[h] = nt(y3s[h], uinv[2]).astype(BF)
+        to_plane(h, 6, x3s.at[h], x3p)
+        yield
         multicast(h, 3, x3s.at[h], xt, 2 * row3 + hi - 16, n2, 16, tp)
         to_output(h, 3, x3s.at[h], row3, n2, 16)
-        yield
-        arrived(xt.at[h, :, 12 * S:16 * S], mc_r.at[h, 3])
-        split(h, nt(cols(xt, h, 12, 16), blocks(12, 14, 28, 32)), psb2, 4)
-        exchange(h, 3, psb2, rbb2)
-        yield
-        acc1[h] = nt(cols(xt, h, 12, 16), blocks(8, 12, 28, 32))
-        acc0[h] = nt(cols(xt, h, 12, 16), blocks(0, 8, 28, 32))
-        g = (y2s[h].astype(F32) - summed(h, 3, psb2, rbb2)).astype(BF)
+        if lead:
+            whole(1, down)
+        arrived(x3p.at[h], mc_r.at[h, 6])
+        g = (y2s[h].astype(F32) - nt(x3p[h], down[...])).astype(BF)
         x2s[h] = nt(g, uinv[1]).astype(BF)
         multicast(h, 4, x2s.at[h], xt, 2 * row2 + hi - 16, n2, 16, tp)
         to_output(h, 2, x2s.at[h], row2, n2, 16)
         yield
+        arrived(xt.at[h, :, 12 * S:16 * S], mc_r.at[h, 3])
+        acc1[h] = nt(cols(xt, h, 12, 16), blocks(8, 12, 28, 32))
+        acc0[h] = nt(cols(xt, h, 12, 16), blocks(0, 8, 28, 32))
         arrived(xt.at[h, :, 8 * S:12 * S], mc_r.at[h, 4])
         split(h, acc1[h] + nt(cols(xt, h, 8, 12), blocks(8, 12, 24, 28)), psb1, 2)
-        exchange(h, 4, psb1, rbb1)
+        exchange(h, 3, psb1, rbb1)
         yield
         acc0[h] += nt(cols(xt, h, 8, 12), blocks(0, 8, 24, 28))
-        g = (y1s[h].astype(F32) - summed(h, 4, psb1, rbb1)).astype(BF)
+        g = (y1s[h].astype(F32) - summed(h, 3, psb1, rbb1)).astype(BF)
         x1s[h] = nt(g, uinv[0]).astype(BF)
         multicast(h, 5, x1s.at[h], xt, 2 * row1 + hi - 16, n1, 32, tp)
         to_output(h, 1, x1s.at[h], row1, n1, 32)
@@ -294,10 +352,10 @@
         for d in range(NP):
             r = level0_row(d)
             ps0[h, d] = part[:, r * S:(r + 1) * S].astype(BF)
-        exchange(h, 5, ps0, rb0)
+        exchange(h, 4, ps0, rb0)
         yield
         arrived(y0own.at[h], yo_r.at[h])
-        g = (y0own[h].astype(F32) - summed(h, 5, ps0, rb0)).astype(BF)
+        g = (y0own[h].astype(F32) - summed(h, 4, ps0, rb0)).astype(BF)
         x0s[h] = nt(g, uinv[3]).astype(BF)
         to_output(h, 0, x0s.at[h], row0, 0, H)
         yield
@@ -354,17 +412,18 @@
         in_specs=[hbm, hbm, pl.BlockSpec(memory_space=pltpu.SMEM), hbm, hbm],
         out_specs=pl.BlockSpec(memory_space=pltpu.VMEM),
         scratch_shapes=[
-            vm(16, 32, S, S), vm(16 * S, 32 * S), vm(2, H, 28 * S), vm(2, H, 16 * S),
+            vm(16, 32, S, S), vm(16 * S, 32 * S), vm(2, H, 24 * S), vm(2, H, 16 * S),
             vm(2 * S, S), vm(2, S, S),
             vm(S, S), vm(2, S, S), vm(2, 32, S), vm(2, 16, S), vm(2, 16, S),
             vm(S, S), vm(3, S, S), vm(4, S, S),
-            vm(2, 8, 32, S), vm(2, 8, 16, S), vm(2, 8, 16, S), vm(2, 8, 16, S), vm(2, 8, 32, S), vm(2, 8, H, S),
-            vm(2, 7, 32, S), vm(2, 7, 16, S), vm(2, 7, 16, S), vm(2, 7, 16, S), vm(2, 7, 32, S), vm(2, 7, H, S),
+            vm(2, 8, 32, S), vm(2, 8, 16, S), vm(2, 8, 16, S), vm(2, 8, 32, S), vm(2, 8, H, S),
+            vm(2, 7, 32, S), vm(2, 7, 16, S), vm(2, 7, 16, S), vm(2, 7, 32, S), vm(2, 7, H, S),
+            vm(S, 32 * S), vm(S, 32 * S), vm(2, 16, 32 * S), vm(2, 16, 32 * S),
             vm(2, H, S), vm(2, 32, S), vm(2, 16, S), vm(2, 16, S),
             vm(2, 16, S), vm(2, 16, S), vm(2, 32, S), vm(2, H, S),
             vm(2, H, S), vm(2, S, S),
             vm(2, H, 4 * S, dtype=F32), vm(2, H, 4 * S, dtype=F32), vm(2, H, 8 * S, dtype=F32),
-            dma, dma((6,)), dma((7,)), dma((2, 6)), dma((2, 6)), dma((2, 6)), dma((2, 6)), dma((2, 6)),
+            dma, dma((6,)), dma((7,)), dma((2,)), dma((2, 4)), dma((2, 5)), dma((2, 5)), dma((2, 7)), dma((2, 7)), dma((2, 7)),
             dma((8,)), dma, dma((2,)), dma, dma, dma((16,)), dma((3,)), dma((2, 8)), dma((2,)), dma((2, 4)), dma,
         ],
         compiler_params=pltpu.CompilerParams(

time: 87.6 us -> 81.3 us (0.928)
  Pallas kernels: 86 us -> 79.6 us
    pallas_call x1, Pallas kernels: 86 us -> 79.6 us  [on_device(): pl.pallas_call(kernel, out_shape=jax.ShapeDtypeStruct(right_sides.shape,...]
where the time goes in v3:
time: 81.3 us; the launch traced here: 81.1 us
  Pallas kernels  79.6 us (98%)
  local copies, waits for them, and re-layouts  1.47 us (2%)
    pallas_call x1, Pallas kernels, on_device(): pl.pallas_call(kernel, out_shape=jax.ShapeDtypeStruct(right_sides.shape,...  79.6 us

profile of v3, /device:TPU:1, one launch (start us, length us, event | category | flops | bytes accessed | tf_op | source)
XLA Modules:
  0.0 81.1 jit_solution(9763312290484768465)
XLA Ops:
  0.0 79.6 %shard_map.55 = bf16[256,128]{1,0:T(8,128)(2,1)} custom-call(bf16[256,128]{1,0:T(8,128)(2,1)} %rhs_hbm.1, bf16[16,32,128,128]{3,2,1,0:T(8,128)(2,1)} %bitcast.4, s32[16,32]{1,0:T(8,128)} %bitcast.7, bf16[16,128,128]{2,1,0:T(8,128)(2,1)} %bitcast.5, bf16[16,128,128]{2,1,0:T(8,128)(2,1)} %bitcast.6), custom_call_target="tpu_custom_call" | custom-call | tf_op jit(solution)/shard_map/pallas_call | solution.py:409
  79.6 1.5 %copy.7 = bf16[256,128]{1,0:T(8,128)(2,1)} copy(bf16[256,128]{1,0:T(8,128)(2,1)} %shard_map.55) | data formatting | bytes 131072

commit v4 on v3

--- a/solution.py
+++ b/solution.py
@@ -29,11 +29,11 @@
 
 
 def kernel(
-    rhs_hbm, factor_hbm, pattern, lower_hbm, upper_hbm, out_ref,
-    raw, fm, yt, xt, rhs_v, rhs_t, b0, bx, b1, b2, b3, linv0, linv, uinv,
+    rhs_hbm, factor_hbm, pattern, lower_hbm, upper_hbm, xo,
+    raw, fm, yt, xt, rhs_v, rhs_t, b0, bx, b1, b2, b3, linv0, lfirst, linv, uinv,
     ps1, ps2, ps3, psb1, ps0, rb1, rb2, rb3, rbb1, rb0, up, down, y2p, x3p,
-    y0s, y1s, y2s, y3s, x3s, x2s, x1s, x0s, y0own, xo, accf, acc1, acc0,
-    lsem, gsem, isem, up_s, up_r, rs_s, rs_r, mc_s, mc_s0, mc_r, l0_s, l0_r, b_s, b0_r, bx_r, bl_s, bl_r, yo_s, yo_r, xo_s, xo_r,
+    y0s, y1s, y2s, y3s, x3s, x2s, x1s, x0s, y0own, accf, acc1, acc0,
+    lsem, fsem, gsem, isem, up_s, up_r, rs_s, rs_r, mc_s, mc_s0, mc_r, l0_s, l0_r, b_s, b0_r, bx_r, bl_s, bl_r, yo_s, yo_r, xo_s, xo_r,
 ):
     p = lax.axis_index("prow")
     q = lax.axis_index("pcol")
@@ -58,6 +58,13 @@
 
     load_rhs = pltpu.make_async_copy(rhs_hbm, rhs_v, lsem)
     load_rhs.start()
+    load_first = pltpu.make_async_copy(lower_hbm.at[0:8], lfirst, fsem)
+    owner = q % NP == p
+
+    @pl.when(owner)
+    def _():
+        load_first.start()
+
     loads = []
     for g, (r0, r1, c0, c1) in enumerate(GROUPS):
         c = pltpu.make_async_copy(factor_hbm.at[r0:r1, c0:c1], raw.at[r0:r1, c0:c1], gsem.at[g])
@@ -75,6 +82,10 @@
     for s in range(2):
         rhs_t[s] = rhs_v[s * S:(s + 1) * S, :].astype(F32).T.astype(BF)
 
+    @pl.when(owner)
+    def _():
+        load_first.wait()
+
     pl.semaphore_wait(
         barrier, 22 + jnp.where(p < 4, 2, 0) - jnp.where(corner, 1, 0)
     )
@@ -103,7 +114,6 @@
         return finish
 
     tp, hi = q % NP, q // NP
-    owner = tp == p
 
     def level0_q(jb):
         return (jb % 4) * 4 + jb // 4
@@ -111,7 +121,7 @@
     @pl.when(owner)
     def _():
         for r in range(8):
-            send(lower_hbm.at[r], linv0, l0_s.at[r], l0_r, p, level0_q(2 * r + hi))
+            send(lfirst.at[r], linv0, l0_s.at[r], l0_r, p, level0_q(2 * r + hi))
 
     for s in range(2):
         @pl.when(p < 4)
@@ -368,10 +378,6 @@
             except StopIteration:
                 chains.remove(c)
 
-    arrived(xo, xo_r)
-    for s in range(2):
-        out_ref[s * S:(s + 1) * S, :] = xo[s].astype(F32).T.astype(BF)
-
     for f in done:
         f()
 
@@ -399,6 +405,8 @@
 
     spread_rhs(True)
 
+    arrived(xo, xo_r)
+
 
 def on_device(right_sides, factor, pattern, lower_inverse, upper_inverse):
     def vm(*shape, dtype=BF):
@@ -406,24 +414,24 @@
 
     dma = pltpu.SemaphoreType.DMA
     hbm = pl.BlockSpec(memory_space=pl.ANY)
-    return pl.pallas_call(
+    solved = pl.pallas_call(
         kernel,
-        out_shape=jax.ShapeDtypeStruct(right_sides.shape, BF),
+        out_shape=jax.ShapeDtypeStruct((2, S, S), BF),
         in_specs=[hbm, hbm, pl.BlockSpec(memory_space=pltpu.SMEM), hbm, hbm],
-        out_specs=pl.BlockSpec(memory_space=pltpu.VMEM),
+        out_specs=hbm,
         scratch_shapes=[
             vm(16, 32, S, S), vm(16 * S, 32 * S), vm(2, H, 24 * S), vm(2, H, 16 * S),
             vm(2 * S, S), vm(2, S, S),
             vm(S, S), vm(2, S, S), vm(2, 32, S), vm(2, 16, S), vm(2, 16, S),
-            vm(S, S), vm(3, S, S), vm(4, S, S),
+            vm(S, S), vm(8, S, S), vm(3, S, S), vm(4, S, S),
             vm(2, 8, 32, S), vm(2, 8, 16, S), vm(2, 8, 16, S), vm(2, 8, 32, S), vm(2, 8, H, S),
             vm(2, 7, 32, S), vm(2, 7, 16, S), vm(2, 7, 16, S), vm(2, 7, 32, S), vm(2, 7, H, S),
             vm(S, 32 * S), vm(S, 32 * S), vm(2, 16, 32 * S), vm(2, 16, 32 * S),
             vm(2, H, S), vm(2, 32, S), vm(2, 16, S), vm(2, 16, S),
             vm(2, 16, S), vm(2, 16, S), vm(2, 32, S), vm(2, H, S),
-            vm(2, H, S), vm(2, S, S),
+            vm(2, H, S),
             vm(2, H, 4 * S, dtype=F32), vm(2, H, 4 * S, dtype=F32), vm(2, H, 8 * S, dtype=F32),
-            dma, dma((6,)), dma((7,)), dma((2,)), dma((2, 4)), dma((2, 5)), dma((2, 5)), dma((2, 7)), dma((2, 7)), dma((2, 7)),
+            dma, dma, dma((6,)), dma((7,)), dma((2,)), dma((2, 4)), dma((2, 5)), dma((2, 5)), dma((2, 7)), dma((2, 7)), dma((2, 7)),
             dma((8,)), dma, dma((2,)), dma, dma, dma((16,)), dma((3,)), dma((2, 8)), dma((2,)), dma((2, 4)), dma,
         ],
         compiler_params=pltpu.CompilerParams(
@@ -436,6 +444,7 @@
         lower_inverse.reshape(16, S, S),
         upper_inverse.reshape(16, S, S),
     )
+    return solved.transpose(0, 2, 1).reshape(right_sides.shape)
 
 
 def solution(mesh):

time: 81.3 us -> 79.6 us (0.979)
  Pallas kernels: 79.6 us -> 77.8 us
    pallas_call x1, Pallas kernels: 79.6 us -> 77.8 us  [on_device(): pl.pallas_call(kernel, out_shape=jax.ShapeDtypeStruct((2, S, S), BF), in_...]
    transpose x0 -> x1, local copies, waits for them, and re-layouts: none -> 1.57 us  [on_device(): return solved.transpose(0, 2, 1).reshape(right_sides.shape)]
    unnamed x1 -> x0, local copies, waits for them, and re-layouts: 1.47 us -> none
where the time goes in v4:
time: 79.6 us; the launch traced here: 79.4 us
  Pallas kernels  77.8 us (98%)
  local copies, waits for them, and re-layouts  1.57 us (2%)
    pallas_call x1, Pallas kernels, on_device(): pl.pallas_call(kernel, out_shape=jax.ShapeDtypeStruct((2, S, S), BF), in_...  77.8 us

profile of v4, /device:TPU:1, one launch (start us, length us, event | category | flops | bytes accessed | tf_op | source)
XLA Modules:
  0.0 79.4 jit_solution(13886652029116255744)
XLA Ops:
  0.0 77.8 %shard_map.55 = bf16[2,128,128]{2,1,0:T(8,128)(2,1)} custom-call(bf16[256,128]{1,0:T(8,128)(2,1)} %rhs_hbm.1, bf16[16,32,128,128]{3,2,1,0:T(8,128)(2,1)} %bitcast.6, s32[16,32]{1,0:T(8,128)} %bitcast.10, bf16[16,128,128]{2,1,0:T(8,128)(2,1)} %bitcast.7, bf16[16,128,128]{2,1,0:T(8,128)(2,1)} %bitcast.8), custom_call_target="tpu_custom_call" | custom-call | tf_op jit(solution)/shard_map/pallas_call | solution.py:417
  77.8 1.6 %copy.6 = bf16[2,128,128]{2,1,0:T(8,128)(2,1)} copy(bf16[2,128,128]{1,2,0:T(8,128)(2,1)} %bitcast.9) | data formatting | bytes 131072 | tf_op jit(solution)/shard_map/transpose | solution.py:447

commit v5 on v4

--- a/solution.py
+++ b/solution.py
@@ -246,10 +246,10 @@
 
     def summed(h, idx, ps, rb):
         arrived(rb.at[h], rs_r.at[h, idx])
-        total = ps[h, p].astype(F32)
-        for k in range(NP - 1):
-            total = total + rb[h, k].astype(F32)
-        return total
+        parts = [ps[h, p].astype(F32)] + [rb[h, k].astype(F32) for k in range(NP - 1)]
+        while len(parts) > 1:
+            parts = [u + v for u, v in zip(parts[::2], parts[1::2])]
+        return parts[0]
 
     def split(h, part, ps, per_row):
         rows = H // per_row
@@ -291,12 +291,6 @@
         split(h, nt(cols(yt, h, 0, 16), blocks(8, 12, 0, 16)), ps1, 2)
         exchange(h, 0, ps1, rb1)
         yield
-        @pl.when(owner)
-        def _():
-            for d in range(NP):
-                col = 2 * level0_row(d) + hi
-                send(yt.at[h, :, pl.ds(pl.multiple_of(col * S, S), S)], y0own.at[h], yo_s.at[h, d], yo_r.at[h], d, q)
-
         accf[h] = nt(cols(yt, h, 0, 16), blocks(12, 16, 0, 16))
         if lead:
             for c in inv_loads:
@@ -305,6 +299,12 @@
         e = (b1[h].astype(F32) - summed(h, 0, ps1, rb1)).astype(BF)
         y1s[h] = nt(e, linv[0]).astype(BF)
         multicast(h, 1, y1s.at[h], yt, 2 * row1 + hi, n1, 32, tp)
+        @pl.when(owner)
+        def _():
+            for d in range(NP):
+                col = 2 * level0_row(d) + hi
+                send(yt.at[h, :, pl.ds(pl.multiple_of(col * S, S), S)], y0own.at[h], yo_s.at[h, d], yo_r.at[h], d, q)
+
         yield
         if lead:
             for g in (4, 5):
@@ -358,11 +358,21 @@
         to_output(h, 1, x1s.at[h], row1, n1, 32)
         yield
         arrived(xt.at[h, :, 0:8 * S], mc_r.at[h, 5])
-        part = acc0[h] + nt(cols(xt, h, 0, 8), blocks(0, 8, 16, 24))
-        for d in range(NP):
-            r = level0_row(d)
-            ps0[h, d] = part[:, r * S:(r + 1) * S].astype(BF)
-        exchange(h, 4, ps0, rb0)
+        for r0 in (0, 4):
+            part = acc0[h, :, r0 * S:(r0 + 4) * S] + nt(cols(xt, h, 0, 8), blocks(r0, r0 + 4, 16, 24))
+            for d in range(NP):
+                r = level0_row(d) - r0
+                if 0 <= r < 4:
+                    ps0[h, d] = part[:, r * S:(r + 1) * S].astype(BF)
+                    k = (d - p + NP) % NP
+
+                    @pl.when(k > 0)
+                    def _():
+                        pltpu.make_async_remote_copy(
+                            src_ref=ps0.at[h, d], dst_ref=rb0.at[h, k - 1], send_sem=rs_s.at[h, 4], recv_sem=rs_r.at[h, 4],
+                            device_id=(d, q), device_id_type=MESH,
+                        ).start()
+        done.append(lambda: arrived(rb0.at[h], rs_s.at[h, 4]))
         yield
         arrived(y0own.at[h], yo_r.at[h])
         g = (y0own[h].astype(F32) - summed(h, 4, ps0, rb0)).astype(BF)

time: 79.6 us -> 78.8 us (0.990)
  no operation moved by 1% of the time
where the time goes in v5:
time: 78.8 us; the launch traced here: 78.6 us
  Pallas kernels  77.1 us (98%)
  local copies, waits for them, and re-layouts  1.57 us (2%)
    pallas_call x1, Pallas kernels, on_device(): pl.pallas_call(kernel, out_shape=jax.ShapeDtypeStruct((2, S, S), BF), in_...  77.1 us

profile of v5, /device:TPU:1, one launch (start us, length us, event | category | flops | bytes accessed | tf_op | source)
XLA Modules:
  0.0 78.6 jit_solution(6142651227100606913)
XLA Ops:
  0.0 77.1 %shard_map.55 = bf16[2,128,128]{2,1,0:T(8,128)(2,1)} custom-call(bf16[256,128]{1,0:T(8,128)(2,1)} %rhs_hbm.1, bf16[16,32,128,128]{3,2,1,0:T(8,128)(2,1)} %bitcast.6, s32[16,32]{1,0:T(8,128)} %bitcast.10, bf16[16,128,128]{2,1,0:T(8,128)(2,1)} %bitcast.7, bf16[16,128,128]{2,1,0:T(8,128)(2,1)} %bitcast.8), custom_call_target="tpu_custom_call" | custom-call | tf_op jit(solution)/shard_map/pallas_call | solution.py:427
  77.1 1.6 %copy.6 = bf16[2,128,128]{2,1,0:T(8,128)(2,1)} copy(bf16[2,128,128]{1,2,0:T(8,128)(2,1)} %bitcast.9) | data formatting | bytes 131072 | tf_op jit(solution)/shard_map/transpose | solution.py:457
